TPU v7x, 256 devices: a whole 4x4x8 slice. The times are simulated.
256 devices in a mesh: row: 8 (over z_hi, x), col: 32 (over y, z_lo, core).
Axes of the slice: x: 4, y: 4, z: 8 (z_hi: 2, z_lo: 4; z = z_hi * 4 + z_lo), core: 2. Of those that a mesh axis runs over, the one named last changes fastest.
Arguments:
- inv_anc: float32 [8, 32, 48, 12288], P(None, 'col', None, 'row'), may hold values from -6 to 6
- factor_cols: float32 [4, 12288, 256], P(None, ('row', 'col')), may hold values from -0.0546875 to 0.0546875
- couple: float32 [6, 256, 256], replicated, may hold values from -0.1875 to 0.1875
- diag_inv: float32 [4, 256, 256], replicated, may hold values from -6 to 6, as said below
- pattern: int32 [4, 48], replicated, may hold values 0 or 1
- parent: int32 [4], replicated, may hold values from 0 to 4, as said below
Outputs:
- inv_cols: float32 [4, 12288, 256], P(None, ('row', 'col'))
- win_cols: float32 [6, 256, 256], replicated
- win_diag: float32 [4, 256, 256], replicated
Inputs may be any that keep to these rules, and one draw needn't show every extreme that they name: parent[0] is 4, meaning a parent in the ancestor set; for j of 1 or more parent[j] is an earlier supernode or 4. Each diag_inv[j] is symmetric.
All inputs are finite; a program needn't handle non-finite values.
Results may differ from a plain program's by a relative error of at most 0.0001.
Values sent between devices are 32-bit elements; how exact they have to be, the bound alone decides.
No kernel may reach another device: no remote copies, remote signals or barrier semaphores. Data moves between devices by JAX's collectives and lax.ppermute only.
A program may use at most 64 MiB of HBM per device.

v0:
```python
import jax
import jax.numpy as jnp
from jax import lax
from jax.sharding import PartitionSpec as P

W = 256
NSUP = 4
exact_mode = lax.Precision.HIGHEST


def product(left, right):
    return jnp.dot(left, right, precision=exact_mode, preferred_element_type=jnp.float32)


def ancestry(parent):
    linked = {}
    for j in range(NSUP):
        for m in range(j):
            linked_now = parent[j] == m
            for p in range(m + 1, j):
                linked_now = linked_now | (parent[j] == p) & linked[p, m]
            linked[j, m] = linked_now
    return linked


def couplings(couple, parent):
    linked = ancestry(parent)
    blocks = {}
    for j in range(NSUP):
        for m in range(j):
            blocks[j, m] = couple[j * (j - 1) // 2 + m] * linked[j, m].astype(jnp.float32)
    return blocks


def window_blocks(crossed, diag_terms, diag_inv, blocks):
    off_diag = {}
    diagonal = []

    def lookup_block(first, second):
        if first == second:
            return diagonal[first]
        if first < second:
            return off_diag[second, first]
        return off_diag[first, second].T

    for j in range(NSUP):
        for m in range(j):
            running = crossed[j, m]
            for q in range(j):
                running = running + product(lookup_block(m, q), blocks[j, q])
            off_diag[j, m] = -running
        diag_value = diag_inv[j] - diag_terms[j]
        for m in range(j):
            diag_value = diag_value - product(blocks[j, m].T, off_diag[j, m])
        diagonal.append(diag_value)
    pair_list = [off_diag[j, m] for j in range(NSUP) for m in range(j)]
    return (jnp.stack(pair_list), jnp.stack(diagonal))


def shards(inv_anc, factor_cols, couple, diag_inv, pattern, parent):
    col_count = lax.axis_size("col")
    local_block = inv_anc.reshape(inv_anc.shape[0] * inv_anc.shape[2], inv_anc.shape[3])
    rows_here = factor_cols.shape[1]
    first_row = (lax.axis_index("row") * col_count + lax.axis_index("col")) * rows_here
    row_ids = first_row + jnp.arange(rows_here, dtype=jnp.int32)
    block_ids = row_ids // W
    one_hot = (block_ids[:, None] == jnp.arange(pattern.shape[1], dtype=jnp.int32)[None, :]).astype(
        jnp.float32
    )
    row_mask = product(one_hot, pattern.astype(jnp.float32).T)
    masked = factor_cols * row_mask.T[:, :, None]
    blocks = couplings(couple, parent)
    columns = []
    for j in range(NSUP):
        partial_value = product(local_block, lax.all_gather(masked[j], "col", axis=0, tiled=True))
        summed = lax.psum_scatter(partial_value, "row", scatter_dimension=0, tiled=True)
        for m in range(j):
            summed = summed + product(columns[m], blocks[j, m])
        columns.append(-summed)
    crossed = {}
    diag_terms = []
    for j in range(NSUP):
        products = [product(columns[m].T, masked[j]) for m in range(j)]
        products.append(product(masked[j].T, columns[j]))
        summed_terms = lax.psum(jnp.stack(products), ("row", "col"))
        for m in range(j):
            crossed[j, m] = summed_terms[m]
        diag_terms.append(summed_terms[j])
    pair_blocks, diagonal = window_blocks(crossed, diag_terms, diag_inv, blocks)
    return (jnp.stack(columns), pair_blocks, diagonal)


def solution(mesh):
    in_specs = (P(None, "col", None, "row"), P(None, ("row", "col"), None), P(), P(), P(), P())
    out_specs = (P(None, ("row", "col"), None), P(), P())
    return jax.shard_map(shards, mesh=mesh, in_specs=in_specs, out_specs=out_specs, check_vma=False)
```

profile of v0, /device:TPU:97, one launch (start us, length us, event | category | flops | bytes accessed | tf_op | source)
XLA Modules:
  0.0 888.4 jit_solution(3892370437769683290)
XLA Ops:
  7.2 1.0 convolution_bitcast_fusion.10
  8.3 1.0 broadcast_multiply_fusion
  9.3 0.7 fusion.117
  10.1 0.7 all-gather.11.cloned.1.call-update
  10.8 0.7 all-gather.13.cloned.1.call-update
  11.5 0.5 all-gather.15.cloned.1.call-update
  12.1 58.4 %all-gather.9.cloned.1.call-done = f32[1,1536,256]{2,1,0:T(8,128)} async-done(((f32[1,48,256]{2,1,0:T(8,128)}), f32[1,1536,256]{2,1,0:T(8,128)}) %all-gather.9.cloned.1.call-update) | async-done | bytes 1572880 | tf_op jit(solution)/shard_map/all_gather | solution.py:75
  70.5 6.5 fusion.8
  77.0 0.9 copy.20
  78.0 52.5 %all-gather.11.cloned.1.call-done = f32[1,1536,256]{2,1,0:T(8,128)} async-done(((f32[1,48,256]{2,1,0:T(8,128)}), f32[1,1536,256]{2,1,0:T(8,128)}) %all-gather.11.cloned.1.call-update) | async-done | bytes 1572880 | tf_op jit(solution)/shard_map/all_gather | solution.py:75
  130.5 6.5 fusion.11
  137.0 0.9 copy.22
  138.2 52.8 %all-gather.13.cloned.1.call-done = f32[1,1536,256]{2,1,0:T(8,128)} async-done(((f32[1,48,256]{2,1,0:T(8,128)}), f32[1,1536,256]{2,1,0:T(8,128)}) %all-gather.13.cloned.1.call-update) | async-done | bytes 1572880 | tf_op jit(solution)/shard_map/all_gather | solution.py:75
  191.1 6.5 fusion.14
  197.5 0.9 copy.24
  198.5 0.6 fusion.118
  202.9 48.6 %all-gather.15.cloned.1.call-done = f32[1,1536,256]{2,1,0:T(8,128)} async-done(((f32[1,48,256]{2,1,0:T(8,128)}), f32[1,1536,256]{2,1,0:T(8,128)}) %all-gather.15.cloned.1.call-update) | async-done | bytes 1572880 | tf_op jit(solution)/shard_map/all_gather | solution.py:75
  251.5 6.5 fusion.17
  258.0 0.9 copy.26
  258.9 0.5 all-reduce.3.cloned.1.call-start
  259.4 76.6 %reduce-scatter.13.cloned.1.call-done = f32[48,256]{1,0:T(8,128)} async-done(((f32[384,256]{1,0:T(8,128)}), f32[48,256]{1,0:T(8,128)}) %reduce-scatter.13.cloned.1.call-update) | async-done | bytes 49168
  336.0 0.9 copy.21
  336.9 84.0 %reduce-scatter.15.cloned.1.call-done = f32[48,256]{1,0:T(8,128)} async-done(((f32[384,256]{1,0:T(8,128)}), f32[48,256]{1,0:T(8,128)}) %reduce-scatter.15.cloned.1.call-update) | async-done | bytes 49168 | tf_op jit(solution)/shard_map/reduce_scatter | solution.py:76
  420.9 1.3 fusion.29
  422.2 83.7 %reduce-scatter.17.cloned.1.call-done = f32[48,256]{1,0:T(8,128)} async-done(((f32[384,256]{1,0:T(8,128)}), f32[48,256]{1,0:T(8,128)}) %reduce-scatter.17.cloned.1.call-update) | async-done | bytes 49168 | tf_op jit(solution)/shard_map/reduce_scatter | solution.py:76
  505.9 1.3 convolution_add_fusion.18
  507.2 1.2 fusion.28
  508.5 1.1 convolution_bitcast_fusion.5
  509.6 1.1 convolution_bitcast_fusion.7
  510.7 1.1 convolution_bitcast_fusion.6
  511.8 1.1 convolution_bitcast_fusion.8
  513.0 1.1 convolution_bitcast_fusion.9
  514.4 1.1 convolution_bitcast_fusion.2
  515.9 1.1 convolution_bitcast_fusion
  517.0 74.6 %reduce-scatter.19.cloned.1.call-done = f32[48,256]{1,0:T(8,128)} async-done(((f32[384,256]{1,0:T(8,128)}), f32[48,256]{1,0:T(8,128)}) %reduce-scatter.19.cloned.1.call-update) | async-done | bytes 49168 | tf_op jit(solution)/shard_map/reduce_scatter | solution.py:76
  591.5 1.4 convolution_add_fusion.17
  592.9 1.2 convolution_add_fusion.15
  594.1 1.2 fusion.27
  595.4 0.4 convolution_bitcast_fusion.4
  595.8 0.8 pad_maximum_fusion.3
  596.7 0.9 pad_maximum_fusion.2
  597.6 1.0 pad_maximum_fusion
  598.8 0.7 pad_maximum_fusion.4
  599.4 267.4 %all-reduce.3.cloned.1.call-done = (f32[2,256,256]{2,1,0:T(8,128)}, f32[1,256,256]{2,1,0:T(8,128)}, f32[3,256,256]{2,1,0:T(8,128)}, f32[4,256,256]{2,1,0:T(8,128)}) async-done(((f32[2,256,256]{2,1,0:T(8,128)}, f32[1,256,256]{2,1,0:T(8,128)}, f32[3,256,256]{2,1,0:T(8,128)}, f32[4,256,256]{2,1,0:T(8,128)}), (f32[2,256,256]{2,1,0:T(8,128)}, f32[1,256,256]{2,1,0:T(8,128)}, f32[3,256,256]{2,1,0:T(8,128)}, ...) | async-done | bytes 2621456 | tf_op jit(solution)/shard_map/psum | solution.py:85
  866.8 1.2 slice_subtract_fusion.3
  868.1 1.5 convolution_add_fusion.12
  869.6 1.3 convolution_add_fusion.8
  870.9 0.4 bitcast_dynamic-update-slice_fusion.5
  871.4 0.6 convolution_subtract_fusion.5
  872.0 0.4 bitcast_dynamic-update-slice_fusion.4
  872.6 0.6 convolution_add_fusion.2
  873.2 0.6 convolution_subtract_fusion.4
  873.8 0.6 convolution_add_fusion.10
  874.4 0.6 convolution_add_fusion.5
  875.8 0.4 bitcast_dynamic-update-slice_fusion.3
  876.2 0.4 bitcast_dynamic-update-slice_fusion.2
  876.6 0.6 convolution_subtract_fusion.2
  877.2 0.6 convolution_subtract_fusion.3
  877.8 0.8 convolution_add_fusion.1
  878.6 0.4 bitcast_dynamic-update-slice_fusion.1
  879.0 0.6 convolution_subtract_fusion.1
  879.6 0.4 bitcast_dynamic-update-slice_fusion
  880.0 0.6 fusion.20
  880.6 1.0 pad_maximum_fusion.1
  (49 shorter events, 2.5 us)
Async XLA Ops:
  7.2 63.3 %copy-start = (f32[8,1,48,1536]{3,2,1,0:T(8,128)S(1)}, f32[8,1,48,1536]{3,2,1,0:T(8,128)}, u32[]{:S(2)}) copy-start(f32[8,1,48,1536]{3,2,1,0:T(8,128)} %param.6) | copy-start | bytes 7077892
  7.2 63.3 %all-gather.9.cloned.1.call-start = ((), (), s32[]{:S(2)}) async-start(), calls=%async_computation.4 | async-start | bytes 1622016 | tf_op jit(solution)/shard_map/all_gather | solution.py:75
  10.0 120.5 %all-gather.11.cloned.1.call-start = ((), (), s32[]{:S(2)}) async-start(), calls=%async_computation.5 | async-start | bytes 1622016 | tf_op jit(solution)/shard_map/all_gather | solution.py:75
  10.8 180.3 %all-gather.13.cloned.1.call-start = ((), (), s32[]{:S(2)}) async-start(), calls=%async_computation.6 | async-start | bytes 1622016 | tf_op jit(solution)/shard_map/all_gather | solution.py:75
  11.5 240.0 %all-gather.15.cloned.1.call-start = ((), (), s32[]{:S(2)}) async-start(), calls=%async_computation.7 | async-start | bytes 1622016 | tf_op jit(solution)/shard_map/all_gather | solution.py:75
  12.1 324.0 %reduce-scatter.13.cloned.1.call-start = ((), (), s32[]{:S(2)}) async-start(), calls=%async_computation.8 | async-start | bytes 442368
  77.9 343.0 %reduce-scatter.15.cloned.1.call-start = ((), (), s32[]{:S(2)}) async-start(), calls=%async_computation.9 | async-start | bytes 442368 | tf_op jit(solution)/shard_map/reduce_scatter | solution.py:76
  137.9 60.6 %copy-start.13 = (s32[4]{0:T(128)S(1)}, s32[4]{0:T(128)}, u32[]{:S(2)}) copy-start(s32[4]{0:T(128)} %param.11) | copy-start | bytes 52
  137.9 368.0 %reduce-scatter.17.cloned.1.call-start = ((), (), s32[]{:S(2)}) async-start(), calls=%async_computation.10 | async-start | bytes 442368 | tf_op jit(solution)/shard_map/reduce_scatter | solution.py:76
  198.5 393.1 %reduce-scatter.19.cloned.1.call-start = ((), (), s32[]{:S(2)}) async-start(), calls=%async_computation.11 | async-start | bytes 442368 | tf_op jit(solution)/shard_map/reduce_scatter | solution.py:76
  258.9 607.9 %all-reduce.3.cloned.1.call-start = ((), (), s32[]{:S(2)}) async-start(), calls=%async_computation.12 | async-start | bytes 5242880 | tf_op jit(solution)/shard_map/psum | solution.py:85
  591.5 4.3 copy-start.6
  591.5 5.1 copy-start.4
  591.5 5.1 copy-start.5
  595.4 2.2 copy-start.7
  595.4 2.2 copy-start.8
  595.4 2.2 copy-start.9
  866.8 2.7 copy-start.1
  866.8 4.1 copy-start.11
  868.0 3.3 copy-start.2
  871.3 1.2 copy-start.3
  871.3 1.8 copy-start.10
  880.0 1.7 copy-start.12
Sparse Core Ops, SparseCore 0:
  10.4 60.0 all-gather.8
  72.4 58.0 all-gather.10
  132.9 58.0 all-gather.12
  193.3 58.0 all-gather.14
  255.8 80.2 reduce-scatter.12
  339.8 81.0 reduce-scatter.14
  424.8 81.1 reduce-scatter.16
  510.4 81.1 reduce-scatter.18
  598.8 267.9 all-reduce.2
where the time goes:
time: 897 us; the launch traced here: 888 us
  waiting for transfers between devices  800 us (89%)
  matrix products  55.6 us (6%)
  between operations  18.2 us (2%)
    psum x1, waiting for transfers between devices, shards(): summed_terms = lax.psum(jnp.stack(products), ('row', 'col'))  267 us
    reduce_scatter x3, waiting for transfers between devices, shards(): lax.psum_scatter(partial_value, 'row', scatter_dimension=0, tiled=True)  242 us
    all_gather x4, waiting for transfers between devices, shards(): lax.all_gather(masked[j], 'col', axis=0, tiled=True)  212 us
    unnamed x10, waiting for transfers between devices  78.6 us
    dot_general x41, matrix products, product(): jnp.dot(left, right, precision=exact_mode, preferred_element_type=jnp.flo...  55.6 us
  transfers between devices with their start and end apart: 9, of which 9 were waited for; matrix products, arithmetic and copies ran while one was open for 5% of the time, Pallas kernels for 0%

commit v1 on v0

--- a/solution.py
+++ b/solution.py
@@ -72,7 +72,12 @@
     blocks = couplings(couple, parent)
     columns = []
     for j in range(NSUP):
-        partial_value = product(local_block, lax.all_gather(masked[j], "col", axis=0, tiled=True))
+        partial_value = product(
+            local_block,
+            jnp.concatenate(
+                lax.all_to_all(jnp.stack([masked[j]] * lax.axis_size("col")), "col", 0, 0), axis=0
+            ),
+        )
         summed = lax.psum_scatter(partial_value, "row", scatter_dimension=0, tiled=True)
         for m in range(j):
             summed = summed + product(columns[m], blocks[j, m])

time: 897 us -> 796 us (0.89)
  waiting for transfers between devices: 800 us -> 554 us
  blocking collectives: 0 us -> 131 us
  starting transfers between devices: 1.08 us -> 15.7 us
    all_gather x4 -> x0, waiting for transfers between devices: 212 us -> none  [shards(): lax.all_gather(masked[j], 'col', axis=0, tiled=True)]
    all_to_all x0 -> x3, blocking collectives: none -> 131 us  [shards(): lax.all_to_all(jnp.stack([masked[j]] * lax.axis_size('col')), 'col', 0, 0)]
    unnamed x10 -> x6, waiting for transfers between devices: 78.6 us -> 33.8 us
    all_to_all x0 -> x1, waiting for transfers between devices: none -> 10.8 us  [shards(): lax.all_to_all(jnp.stack([masked[j]] * lax.axis_size('col')), 'col', 0, 0)]
  transfers between devices with their start and end apart: 9 -> 6, of which waited for: 9 -> 6; matrix products, arithmetic and copies ran while one was open for 5% -> 6% of each run, Pallas kernels for 0% -> 0%
where the time goes in v1:
time: 796 us; the launch traced here: 789 us
  waiting for transfers between devices  554 us (70%)
  blocking collectives  131 us (16%)
  matrix products  55.6 us (7%)
  between operations  18.3 us (2%)
  starting transfers between devices  15.7 us (2%)
    psum x1, waiting for transfers between devices, shards(): summed_terms = lax.psum(jnp.stack(products), ('row', 'col'))  268 us
    reduce_scatter x3, waiting for transfers between devices, shards(): lax.psum_scatter(partial_value, 'row', scatter_dimension=0, tiled=True)  242 us
    all_to_all x3, blocking collectives, shards(): lax.all_to_all(jnp.stack([masked[j]] * lax.axis_size('col')), 'col', 0, 0)  131 us
    dot_general x41, matrix products, product(): jnp.dot(left, right, precision=exact_mode, preferred_element_type=jnp.flo...  55.6 us
    unnamed x6, waiting for transfers between devices  33.8 us
  transfers between devices with their start and end apart: 6, of which 6 were waited for; matrix products, arithmetic and copies ran while one was open for 6% of the time, Pallas kernels for 0%

profile of v1, /device:TPU:97, one launch (start us, length us, event | category | flops | bytes accessed | tf_op | source)
XLA Modules:
  0.0 789.3 jit_solution(14796008503216314915)
XLA Ops:
  7.2 1.0 convolution_bitcast_fusion.14
  8.2 1.0 broadcast_multiply_fusion
  9.5 45.3 %all_to_all.20 = f32[32,48,256]{2,1,0:T(8,128)} all-to-all(f32[32,48,256]{2,1,0:T(8,128)S(1)} %stack.104), channel_id=1, replica_groups=mesh['row'=8,'col'=32] {'col'}, dimensions={0} | all-to-all | bytes 3145728 | tf_op jit(solution)/shard_map/all_to_all | solution.py:78
  54.9 42.9 %all_to_all.21 = f32[32,48,256]{2,1,0:T(8,128)} all-to-all(f32[32,48,256]{2,1,0:T(8,128)S(1)} %stack.102), channel_id=1, replica_groups=mesh['row'=8,'col'=32] {'col'}, dimensions={0} | all-to-all | bytes 3145728 | tf_op jit(solution)/shard_map/all_to_all | solution.py:78
  98.0 42.9 %all_to_all.22 = f32[32,48,256]{2,1,0:T(8,128)} all-to-all(f32[32,48,256]{2,1,0:T(8,128)S(1)} %stack.100), channel_id=1, replica_groups=mesh['row'=8,'col'=32] {'col'}, dimensions={0} | all-to-all | bytes 3145728 | tf_op jit(solution)/shard_map/all_to_all | solution.py:78
  140.9 1.3 stack.106
  142.2 6.5 all-to-all-start.3
  148.7 6.5 convolution_bitcast_fusion.3
  155.2 0.9 copy.20
  156.1 0.4 reduce-scatter.15.cloned.1.call-start
  156.6 6.5 convolution_bitcast_fusion.2
  163.0 0.9 copy.22
  164.0 6.5 convolution_bitcast_fusion.1
  170.5 0.9 copy.24
  171.5 0.6 fusion.77
  176.0 10.8 %all-to-all-done.3 = f32[32,48,256]{2,1,0:T(8,128)} async-done(((f32[32,48,256]{2,1,0:T(8,128)}), f32[32,48,256]{2,1,0:T(8,128)}, u32[]{:S(2)}, u32[]{:S(2)}) %all-to-all-start.3) | async-done | bytes 1572896 | tf_op jit(solution)/shard_map/all_to_all | solution.py:78
  186.9 6.5 convolution_bitcast_fusion
  193.4 0.9 copy.26
  194.3 8.7 %all-reduce.3.cloned.1.call-start = ((), (), s32[]{:S(2)}) async-start(), calls=%async_computation.12 | async-start | bytes 5242880 | tf_op jit(solution)/shard_map/psum | solution.py:90
  203.0 33.7 %reduce-scatter.13.cloned.1.call-done = f32[48,256]{1,0:T(8,128)} async-done(((f32[384,256]{1,0:T(8,128)}), f32[48,256]{1,0:T(8,128)}) %reduce-scatter.13.cloned.1.call-update) | async-done | bytes 49168
  236.7 0.9 copy.21
  237.6 84.1 %reduce-scatter.15.cloned.1.call-done = f32[48,256]{1,0:T(8,128)} async-done(((f32[384,256]{1,0:T(8,128)}), f32[48,256]{1,0:T(8,128)}) %reduce-scatter.15.cloned.1.call-update) | async-done | bytes 49168 | tf_op jit(solution)/shard_map/reduce_scatter | solution.py:81
  321.8 1.3 fusion.9
  323.1 83.7 %reduce-scatter.17.cloned.1.call-done = f32[48,256]{1,0:T(8,128)} async-done(((f32[384,256]{1,0:T(8,128)}), f32[48,256]{1,0:T(8,128)}) %reduce-scatter.17.cloned.1.call-update) | async-done | bytes 49168 | tf_op jit(solution)/shard_map/reduce_scatter | solution.py:81
  406.8 1.3 convolution_add_fusion.18
  408.1 1.2 fusion.8
  409.3 1.1 convolution_bitcast_fusion.9
  410.4 1.1 convolution_bitcast_fusion.11
  411.5 1.1 convolution_bitcast_fusion.10
  412.7 1.1 convolution_bitcast_fusion.12
  413.8 1.1 convolution_bitcast_fusion.13
  415.3 1.1 convolution_bitcast_fusion.6
  416.7 1.1 convolution_bitcast_fusion.4
  417.8 74.4 %reduce-scatter.19.cloned.1.call-done = f32[48,256]{1,0:T(8,128)} async-done(((f32[384,256]{1,0:T(8,128)}), f32[48,256]{1,0:T(8,128)}) %reduce-scatter.19.cloned.1.call-update) | async-done | bytes 49168 | tf_op jit(solution)/shard_map/reduce_scatter | solution.py:81
  492.2 1.4 convolution_add_fusion.17
  493.6 1.2 convolution_add_fusion.15
  494.8 1.2 fusion.7
  496.1 0.4 convolution_bitcast_fusion.8
  496.5 0.8 pad_maximum_fusion.3
  497.3 0.9 pad_maximum_fusion.2
  498.3 1.0 pad_maximum_fusion
  499.4 0.7 pad_maximum_fusion.4
  500.1 267.5 %all-reduce.3.cloned.1.call-done = (f32[2,256,256]{2,1,0:T(8,128)}, f32[1,256,256]{2,1,0:T(8,128)}, f32[3,256,256]{2,1,0:T(8,128)}, f32[4,256,256]{2,1,0:T(8,128)}) async-done(((f32[2,256,256]{2,1,0:T(8,128)}, f32[1,256,256]{2,1,0:T(8,128)}, f32[3,256,256]{2,1,0:T(8,128)}, f32[4,256,256]{2,1,0:T(8,128)}), (f32[2,256,256]{2,1,0:T(8,128)}, f32[1,256,256]{2,1,0:T(8,128)}, f32[3,256,256]{2,1,0:T(8,128)}, ...) | async-done | bytes 2621456 | tf_op jit(solution)/shard_map/psum | solution.py:90
  767.7 1.2 slice_subtract_fusion.3
  768.9 1.5 convolution_add_fusion.12
  770.4 1.3 convolution_add_fusion.8
  771.8 0.4 bitcast_dynamic-update-slice_fusion.5
  772.2 0.6 convolution_subtract_fusion.5
  772.8 0.4 bitcast_dynamic-update-slice_fusion.4
  773.4 0.6 convolution_add_fusion.2
  774.0 0.6 convolution_subtract_fusion.4
  774.6 0.6 convolution_add_fusion.10
  775.2 0.6 convolution_add_fusion.5
  776.2 0.4 convolution_add_fusion.4
  776.6 0.4 bitcast_dynamic-update-slice_fusion.3
  777.0 0.4 bitcast_dynamic-update-slice_fusion.2
  777.4 0.6 convolution_subtract_fusion.2
  778.0 0.6 convolution_subtract_fusion.3
  778.6 0.8 convolution_add_fusion.1
  779.4 0.4 bitcast_dynamic-update-slice_fusion.1
  779.8 0.6 convolution_subtract_fusion.1
  780.4 0.4 bitcast_dynamic-update-slice_fusion
  780.8 0.6 fusion
  781.5 1.0 pad_maximum_fusion.1
  (46 shorter events, 2.2 us)
Async XLA Ops:
  7.2 141.5 %copy-start = (f32[8,1,48,1536]{3,2,1,0:T(8,128)S(1)}, f32[8,1,48,1536]{3,2,1,0:T(8,128)}, u32[]{:S(2)}) copy-start(f32[8,1,48,1536]{3,2,1,0:T(8,128)} %param.6) | copy-start | bytes 7077892
  142.2 44.7 %all-to-all-start.3 = ((f32[32,48,256]{2,1,0:T(8,128)}), f32[32,48,256]{2,1,0:T(8,128)}, u32[]{:S(2)}, u32[]{:S(2)}) async-start(f32[32,48,256]{2,1,0:T(8,128)} %stack.106), calls=%async_computation.3 | async-start | bytes 3145728 | tf_op jit(solution)/shard_map/all_to_all | solution.py:78
  148.6 88.1 %reduce-scatter.13.cloned.1.call-start = ((), (), s32[]{:S(2)}) async-start(), calls=%async_computation.8 | async-start | bytes 442368
  156.1 165.6 %reduce-scatter.15.cloned.1.call-start = ((), (), s32[]{:S(2)}) async-start(), calls=%async_computation.9 | async-start | bytes 442368 | tf_op jit(solution)/shard_map/reduce_scatter | solution.py:81
  164.0 242.8 %reduce-scatter.17.cloned.1.call-start = ((), (), s32[]{:S(2)}) async-start(), calls=%async_computation.10 | async-start | bytes 442368 | tf_op jit(solution)/shard_map/reduce_scatter | solution.py:81
  164.0 7.5 copy-start.13
  171.5 320.7 %reduce-scatter.19.cloned.1.call-start = ((), (), s32[]{:S(2)}) async-start(), calls=%async_computation.11 | async-start | bytes 442368 | tf_op jit(solution)/shard_map/reduce_scatter | solution.py:81
  194.3 573.4 %all-reduce.3.cloned.1.call-start = ((), (), s32[]{:S(2)}) async-start(), calls=%async_computation.12 | async-start | bytes 5242880 | tf_op jit(solution)/shard_map/psum | solution.py:90
  492.2 4.3 copy-start.6
  492.2 5.1 copy-start.4
  492.2 5.1 copy-start.5
  496.0 2.2 copy-start.7
  496.0 2.2 copy-start.8
  496.1 2.2 copy-start.9
  767.7 2.7 copy-start.1
  767.7 4.1 copy-start.11
  768.9 3.3 copy-start.2
  772.2 1.2 copy-start.3
  772.2 1.8 copy-start.10
  780.8 1.7 copy-start.12
Sparse Core Ops, SparseCore 0:
  156.2 80.4 reduce-scatter.12
  240.6 81.1 reduce-scatter.14
  325.6 81.0 reduce-scatter.16
  411.1 81.0 reduce-scatter.18
  499.5 268.1 all-reduce.2
